TPU v7x, 32 devices: a whole 2x2x4 slice. The times are simulated.
32 devices in a mesh: groups: 2 (over y), tok: 16 (over z, x, core).
Axes of the slice: x: 2, y: 2, z: 4, core: 2. Of those that a mesh axis runs over, the one named last changes fastest.
Arguments:
- queries: bfloat16 [1024, 2048], P(('groups', 'tok')), parts along dimension 0, may hold values from -6 to 6
- new_kv: bfloat16 [3072, 4096], P(('groups', 'tok')), parts along dimension 0, may hold values from -6 to 6
- prev_kv: bfloat16 [2, 3072, 4096], P(None, ('groups', 'tok')), parts along dimension 1, may hold values from -6 to 6
- base_step: int32 [32], P(('groups', 'tok')), parts along dimension 0, may hold values from 0 to 1
- live_counts: int32 [32], P('groups'), parts along dimension 0, may hold values from 1 to 96
- sketch: float32 [4096, 32], replicated, may hold values from -0.09375 to 0.09375
- cache: bfloat16 [64, 1536, 128], P(('groups', 'tok')), parts along dimension 0, may hold values from -6 to 6, as said below
- w_out: bfloat16 [2048, 1536], replicated, may hold values from -0.125 to 0.125
Outputs:
- projected: bfloat16 [1024, 1536], P(('groups', 'tok')), parts along dimension 0
There are 2 independent parts, one for each index of `groups`. A program takes and returns all parts, laid end to end along the dimension named above; an argument that names none is the same for every part. Nothing has to cross between parts.
Inputs may be any that keep to these rules, and one draw needn't show every extreme that they name: cache slots i and j hold the same values when i // 2 == j // 2 and i % 2 == j % 2.
All inputs are finite; a program needn't handle non-finite values.
Results may differ from a plain program's by a relative error of at most 0.019.
Values may be sent and summed in bfloat16 or wider, within the bound.
No kernel may reach another device: no remote copies, remote signals or barrier semaphores. Data moves between devices by JAX's collectives and lax.ppermute only.
A program may use at most 128 MiB of HBM per device.

v0:
```python
import math

import jax
import jax.numpy as jnp
from jax import lax
from jax.sharding import PartitionSpec as P

HD = 64
SWEEPS = 2


highest = lax.Precision.HIGHEST


def orthonormal(block_cols):
    gram_matrix = jnp.dot(block_cols.T, block_cols, precision=highest)
    lower_factor = jnp.linalg.cholesky(gram_matrix)
    return jax.scipy.linalg.solve_triangular(lower_factor, block_cols.T, lower=True).T


def compress(delta_block, sketch):
    basis_cols = orthonormal(jnp.dot(delta_block, sketch, precision=highest))
    for sweep_index in range(SWEEPS):
        inner = jnp.dot(delta_block.T, basis_cols, precision=highest)
        basis_cols = orthonormal(jnp.dot(delta_block, inner, precision=highest))
    right_factor = jnp.dot(basis_cols.T, delta_block, precision=highest)
    return (basis_cols.astype(jnp.bfloat16), right_factor.astype(jnp.bfloat16))


def spread_heads(matrix, head_groups, groups_q, width):
    lead = matrix.shape[0]
    per_group = matrix.reshape(lead, head_groups, width).transpose(1, 0, 2)
    copies = jnp.broadcast_to(per_group[:, None], (head_groups, groups_q, lead, width))
    return copies.reshape(head_groups * groups_q, lead, width)


def attend_head(pieces, live_keys):
    q_head, keys_values = pieces
    key_part = keys_values[:, :HD]
    value_part = keys_values[:, HD:]
    query_count = q_head.shape[0]
    block_rows = math.gcd(query_count, 512)

    def one_block(query_block):
        scores = jnp.dot(query_block, key_part.T, preferred_element_type=jnp.float32) * HD ** (-0.5)
        scores = jnp.where(live_keys[None, :], scores, -1e30)
        row_max = jnp.max(scores, axis=-1, keepdims=True)
        exponent = jnp.exp(scores - row_max)
        weights = (exponent / jnp.sum(exponent, axis=-1, keepdims=True)).astype(jnp.bfloat16)
        return jnp.dot(weights, value_part, preferred_element_type=jnp.float32).astype(jnp.bfloat16)

    return lax.map(one_block, q_head.reshape(query_count // block_rows, block_rows, HD)).reshape(
        query_count, HD
    )


def per_device(queries, new_kv, prev_kv, base_step, live_counts, sketch, cache, w_out):
    shards = lax.axis_size("tok")
    tok_rows = new_kv.shape[0]
    query_rows = queries.shape[0]
    head_count = queries.shape[1] // HD
    groups_q = max(1, shards // head_count)
    per_dev = head_count * groups_q // shards
    head_groups = head_count // per_dev
    part_rows = query_rows // groups_q
    width = per_dev * 2 * HD
    key_count = shards * tok_rows
    query_count = shards * part_rows
    prior = prev_kv[0].astype(jnp.float32)
    prior = jnp.where(base_step[0] == 1, prev_kv[1].astype(jnp.float32), prior)
    delta = new_kv.astype(jnp.float32) - prior
    left_factor, right_factor = compress(delta, sketch)
    rank_cols = left_factor.shape[1]
    q_blocks = queries.reshape(groups_q, part_rows, head_groups, per_dev * HD)
    q_blocks = q_blocks.transpose(2, 0, 1, 3).reshape(shards, part_rows, per_dev * HD)
    w_blocks = spread_heads(right_factor, head_groups, groups_q, width)
    q_here = lax.all_to_all(q_blocks, "tok", split_axis=0, concat_axis=0, tiled=True)
    u_here = lax.all_gather(left_factor, "tok", axis=0, tiled=True).reshape(
        shards, tok_rows, rank_cols
    )
    w_here = lax.all_to_all(w_blocks, "tok", split_axis=0, concat_axis=0, tiled=True)
    lowrank = jnp.einsum("str,src->stc", u_here, w_here, preferred_element_type=jnp.float32).astype(
        jnp.bfloat16
    )
    lowrank = lowrank.reshape(key_count, per_dev, 2 * HD).transpose(1, 0, 2)
    keys_values = (cache.astype(jnp.float32) + lowrank.astype(jnp.float32)).astype(jnp.bfloat16)
    live_keys = (jnp.arange(tok_rows, dtype=jnp.int32)[None, :] < live_counts[:, None]).reshape(
        key_count
    )
    q_heads = q_here.reshape(query_count, per_dev, HD).transpose(1, 0, 2)
    attended = lax.map(lambda pieces: attend_head(pieces, live_keys), (q_heads, keys_values))
    attended = attended.transpose(1, 0, 2).reshape(shards, part_rows, per_dev * HD)
    returned = lax.all_to_all(attended, "tok", split_axis=0, concat_axis=0, tiled=True)
    returned = returned.reshape(head_groups, groups_q, part_rows, per_dev * HD)
    row_block = returned.transpose(1, 2, 0, 3).reshape(query_rows, head_count * HD)
    return jnp.dot(row_block, w_out, preferred_element_type=jnp.float32).astype(jnp.bfloat16)


def solution(mesh):
    return jax.shard_map(
        per_device,
        mesh=mesh,
        in_specs=(
            P(("groups", "tok"), None),
            P(("groups", "tok"), None),
            P(None, ("groups", "tok"), None),
            P(("groups", "tok")),
            P("groups"),
            P(),
            P(("groups", "tok"), None, None),
            P(),
        ),
        out_specs=P(("groups", "tok"), None),
        check_vma=False,
    )
```

profile of v0, /device:TPU:0, one launch (start us, length us, event | category | flops | bytes accessed | tf_op | source)
XLA Modules:
  0.0 94.7 jit_solution(8483638808945009714)
XLA Ops:
  0.0 1.0 %copy.33 = bf16[4,8,16,128]{3,2,1,0:T(8,128)(2,1)S(1)} copy(bf16[4,8,16,128]{3,1,2,0:T(8,128)(2,1)} %bitcast.116) | data formatting | bytes 262144
  1.0 0.7 copy.43
  1.7 7.4 %all-to-all-start = ((bf16[16,32,128]{2,1,0:T(8,128)(2,1)}), bf16[16,32,128]{2,1,0:T(8,128)(2,1)S(1)}, u32[]{:S(2)}, u32[]{:S(2)}) async-start(bf16[16,32,128]{2,1,0:T(8,128)(2,1)} %bitcast.103), calls=%async_computation | async-start | bytes 262144 | tf_op jit(solution)/shard_map/all_to_all | solution.py:77
  9.7 1.9 %bitcast_subtract_fusion = f32[96,4096]{1,0:T(8,128)S(1)} fusion(bf16[96,4096]{1,0:T(8,128)(2,1)} %param.14, bf16[2,96,4096]{2,1,0:T(8,128)(2,1)} %param.15, pred[]{:T(512)} %bitcast.3), kind=kLoop, calls=%fused_computation.21 | loop fusion | flops 1966080 | bytes 3932161 | tf_op jit(solution)/shard_map/sub | solution.py:71
  11.6 1.3 %fusion.37 = f32[96,32]{0,1:T(8,128)S(1)} fusion(f32[96,4096]{1,0:T(8,128)S(1)} %bitcast_subtract_fusion, f32[4096,32]{0,1:T(8,128)S(1)} %copy-done), kind=kOutput, calls=%fused_computation.61 | convolution fusion | flops 150994944 | bytes 2109440 | tf_op jit(solution)/shard_map/dot_general | solution.py:22
  13.0 0.1 fusion.38
  13.2 2.9 %cholesky.59 = f32[32,32]{1,0:T(8,128)S(1)} custom-call(f32[32,32]{1,0:T(8,128)S(1)} %fusion.31), custom_call_target="Cholesky" | custom-call | tf_op jit(solution)/shard_map/jit(cholesky)/cholesky | solution.py:17
  16.2 0.6 compare_reduce_fusion.2
  16.8 0.7 fusion.17
  17.5 2.4 %custom-call.7 = f32[1,32,32]{1,2,0:T(8,128)S(1)} custom-call(f32[1,32,32]{2,1,0:T(8,128)S(1)} %fusion.17), custom_call_target="InvertDiagBlocksLowerTriangular" | custom-call | tf_op jit(solution)/shard_map/jit(_solve_triangular)/triangular_solve | solution.py:18
  19.9 0.2 fusion.28
  20.1 1.0 %fusion.39 = f32[4096,32]{0,1:T(8,128)S(1)} fusion(f32[96,4096]{1,0:T(8,128)S(1)} %bitcast_subtract_fusion, f32[32,96]{1,0:T(8,128)S(1)} %fusion.28), kind=kOutput, calls=%fused_computation.63 | convolution fusion | flops 150994944 | bytes 2109440 | tf_op jit(solution)/shard_map/dot_general | solution.py:24
  21.2 1.3 %fusion.40 = f32[96,32]{0,1:T(8,128)S(1)} fusion(f32[96,4096]{1,0:T(8,128)S(1)} %bitcast_subtract_fusion, f32[4096,32]{0,1:T(8,128)S(1)} %fusion.39), kind=kOutput, calls=%fused_computation.64 | convolution fusion | flops 150994944 | bytes 2109440 | tf_op jit(solution)/shard_map/dot_general | solution.py:25
  22.5 0.1 fusion.41
  22.7 2.9 %cholesky.70 = f32[32,32]{1,0:T(8,128)S(1)} custom-call(f32[32,32]{1,0:T(8,128)S(1)} %fusion.27), custom_call_target="Cholesky" | custom-call | tf_op jit(solution)/shard_map/jit(cholesky)/cholesky | solution.py:17
  25.7 0.6 compare_reduce_fusion.1
  26.3 0.7 fusion.18
  27.0 2.4 %custom-call.8 = f32[1,32,32]{1,2,0:T(8,128)S(1)} custom-call(f32[1,32,32]{2,1,0:T(8,128)S(1)} %fusion.18), custom_call_target="InvertDiagBlocksLowerTriangular" | custom-call | tf_op jit(solution)/shard_map/jit(_solve_triangular)/triangular_solve | solution.py:18
  29.4 0.2 fusion.24
  29.7 1.0 %fusion.42 = f32[4096,32]{0,1:T(8,128)S(1)} fusion(f32[96,4096]{1,0:T(8,128)S(1)} %bitcast_subtract_fusion, f32[32,96]{1,0:T(8,128)S(1)} %fusion.24), kind=kOutput, calls=%fused_computation.66 | convolution fusion | flops 150994944 | bytes 2109440 | tf_op jit(solution)/shard_map/dot_general | solution.py:24
  30.7 1.3 %fusion.43 = f32[96,32]{0,1:T(8,128)S(1)} fusion(f32[96,4096]{1,0:T(8,128)S(1)} %bitcast_subtract_fusion, f32[4096,32]{0,1:T(8,128)S(1)} %fusion.42), kind=kOutput, calls=%fused_computation.67 | convolution fusion | flops 150994944 | bytes 2109440 | tf_op jit(solution)/shard_map/dot_general | solution.py:25
  32.0 0.1 fusion.44
  32.3 2.9 %cholesky.81 = f32[32,32]{1,0:T(8,128)S(1)} custom-call(f32[32,32]{1,0:T(8,128)S(1)} %fusion.23), custom_call_target="Cholesky" | custom-call | tf_op jit(solution)/shard_map/jit(cholesky)/cholesky | solution.py:17
  35.2 0.6 compare_reduce_fusion
  35.9 0.7 fusion.19
  36.5 2.4 %custom-call.9 = f32[1,32,32]{1,2,0:T(8,128)S(1)} custom-call(f32[1,32,32]{2,1,0:T(8,128)S(1)} %fusion.19), custom_call_target="InvertDiagBlocksLowerTriangular" | custom-call | tf_op jit(solution)/shard_map/jit(_solve_triangular)/triangular_solve | solution.py:18
  39.0 0.2 fusion.20
  39.2 0.9 convolution_convert_fusion
  40.1 0.7 copy.42
  40.8 6.0 %all-to-all-start.1 = ((bf16[16,32,256]{2,1,0:T(8,128)(2,1)}), bf16[16,32,256]{2,1,0:T(8,128)(2,1)S(1)}, u32[]{:S(2)}, u32[]{:S(2)}) async-start(bf16[16,32,256]{2,1,0:T(8,128)(2,1)} %bitcast.102), calls=%async_computation.1 | async-start | bytes 524288 | tf_op jit(solution)/shard_map/all_to_all | solution.py:81
  46.8 22.3 %all-gather = bf16[16,96,32]{1,2,0:T(8,128)(2,1)S(1)} all-gather(bf16[1,96,32]{1,2,0:T(8,128)(2,1)S(1)} %convert_bitcast_fusion), channel_id=1, replica_groups=mesh['groups'=2,'tok'=16] {'tok'}, dimensions={0}, use_global_device_ids=true | all-gather | bytes 104448 | tf_op jit(solution)/shard_map/all_gather | solution.py:78
  69.2 0.1 reshape.49
  69.4 1.6 %fusion.14 = f32[16,96,256]{2,1,0:T(8,128)} fusion(bf16[16,96,32]{1,2,0:T(8,128)(2,1)S(1)} %all-gather, bf16[16,32,256]{2,1,0:T(8,128)(2,1)S(1)} %all-to-all-done.1), kind=kOutput, calls=%fused_computation.23 | convolution fusion | flops 25952256 | bytes 1933312 | tf_op jit(solution)/shard_map/str,src->stc/dot_general | solution.py:82
  71.0 2.1 %reshape.55 = f32[1536,2,128]{2,1,0:T(2,128)S(1)} reshape(f32[16,96,256]{2,1,0:T(8,128)} %fusion.14) | data formatting | bytes 3145728 | tf_op jit(solution)/shard_map/convert_element_type | solution.py:86
  73.0 1.3 %fusion.13 = bf16[2,1536,128]{2,1,0:T(8,128)(2,1)S(1)} fusion(f32[1536,2,128]{2,1,0:T(2,128)S(1)} %reshape.55, bf16[2,1536,128]{2,1,0:T(8,128)(2,1)} %param.19), kind=kLoop, calls=%fused_computation.20 | loop fusion | flops 1179648 | bytes 3145728 | tf_op jit(solution)/shard_map/convert_element_type | solution.py:86
  74.3 4.9 %while.11 = (s32[]{:T(128)}, bf16[2,512,64]{1,2,0:T(8,128)(2,1)S(1)}, bf16[2,512,64]{2,1,0:T(8,128)(2,1)S(1)}, bf16[2,1536,128]{2,1,0:T(8,128)(2,1)S(1)}, s32[16]{0:T(128)S(1)}, /*index=5*/s32[]{:T(128)}) while((s32[]{:T(128)}, bf16[2,512,64]{1,2,0:T(8,128)(2,1)S(1)}, bf16[2,512,64]{2,1,0:T(8,128)(2,1)S(1)}, ...), condition=%wide.region_5.8_spmd.clone, body=%wide.region_2.7_spmd.clone.sunk | while | flops 207651328 | bytes 11223697 | solution.py:91
  74.5 0.1 broadcast_in_dim.43
  74.5 0.7 fusion.71
  75.2 0.6 fusion.72
  75.8 1.0 %fusion.73 = bf16[2,512,64]{1,2,0:T(8,128)(2,1)S(1)} fusion(bf16[2,512,64]{1,2,0:T(8,128)(2,1)S(1)} %get-tuple-element.130, s32[]{:T(128)} %get-tuple-element.129, f32[512,1536]{1,0:T(8,128)S(1)} %get-tuple-element.121, f32[512]{0:T(512)S(1)} %fusion.72, f32[512]{0:T(512)S(1)} %get-tuple-element.122, ...), kind=kOutput, calls=%fused_computation.9.clone.1 | convolution fusion | flops 103055360 | bytes 3608580 | tf_op jit(solution)/shard_map/while/body/eval_jaxpr/while/body/eval_jaxpr/dot_general | solution.py:50
  76.9 0.1 broadcast_in_dim.43
  77.0 0.7 fusion.71
  77.7 0.6 fusion.72
  78.3 1.0 %fusion.73 = bf16[2,512,64]{1,2,0:T(8,128)(2,1)S(1)} fusion(bf16[2,512,64]{1,2,0:T(8,128)(2,1)S(1)} %get-tuple-element.130, s32[]{:T(128)} %get-tuple-element.129, f32[512,1536]{1,0:T(8,128)S(1)} %get-tuple-element.121, f32[512]{0:T(512)S(1)} %fusion.72, f32[512]{0:T(512)S(1)} %get-tuple-element.122, ...), kind=kOutput, calls=%fused_computation.9.clone.1 | convolution fusion | flops 103055360 | bytes 3608580 | tf_op jit(solution)/shard_map/while/body/eval_jaxpr/while/body/eval_jaxpr/dot_general | solution.py:50
  79.3 0.2 copy.30
  79.4 0.1 reshape.52
  79.6 10.5 %all_to_all.15 = bf16[16,32,128]{2,1,0:T(8,128)(2,1)S(1)} all-to-all(bf16[16,32,128]{2,1,0:T(8,128)(2,1)S(1)} %reshape.52), channel_id=1, replica_groups=mesh['groups'=2,'tok'=16] {'tok'}, dimensions={0} | all-to-all | bytes 262144 | tf_op jit(solution)/shard_map/all_to_all | solution.py:93
  90.1 4.6 %convolution_convert_fusion.1 = bf16[32,1536]{1,0:T(8,128)(2,1)} fusion(bf16[2048,1536]{1,0:T(8,128)(2,1)} %param.20, bf16[4,8,16,128]{3,2,1,0:T(8,128)(2,1)S(1)} %bitcast.112), kind=kOutput, calls=%fused_computation.18 | convolution fusion | flops 201375744 | bytes 6520832 | tf_op jit(solution)/shard_map/dot_general | solution.py:96
  (23 shorter events, 0.7 us)
Async XLA Ops:
  0.0 11.6 %copy-start = (f32[4096,32]{0,1:T(8,128)S(1)}, f32[4096,32]{0,1:T(8,128)}, u32[]{:S(2)}) copy-start(f32[4096,32]{0,1:T(8,128)} %param.18) | copy-start | bytes 1572868
  1.7 39.1 %all-to-all-start = ((bf16[16,32,128]{2,1,0:T(8,128)(2,1)}), bf16[16,32,128]{2,1,0:T(8,128)(2,1)S(1)}, u32[]{:S(2)}, u32[]{:S(2)}) async-start(bf16[16,32,128]{2,1,0:T(8,128)(2,1)} %bitcast.103), calls=%async_computation | async-start | bytes 262144 | tf_op jit(solution)/shard_map/all_to_all | solution.py:77
  40.8 28.6 %all-to-all-start.1 = ((bf16[16,32,256]{2,1,0:T(8,128)(2,1)}), bf16[16,32,256]{2,1,0:T(8,128)(2,1)S(1)}, u32[]{:S(2)}, u32[]{:S(2)}) async-start(bf16[16,32,256]{2,1,0:T(8,128)(2,1)} %bitcast.102), calls=%async_computation.1 | async-start | bytes 524288 | tf_op jit(solution)/shard_map/all_to_all | solution.py:81
  73.0 1.3 %copy-start.1 = (s32[16]{0:T(128)S(1)}, s32[16]{0:T(128)}, u32[]{:S(2)}) copy-start(s32[16]{0:T(128)} %param.17) | copy-start | bytes 196
where the time goes:
time: 95.2 us; the launch traced here: 94.7 us
  blocking collectives  32.8 us (34%)
  other arithmetic  24.6 us (26%)
  matrix products  17.5 us (18%)
  starting transfers between devices  13.4 us (14%)
  local copies, waits for them, and re-layouts  5.45 us (6%)
    all_gather x1, blocking collectives, per_device(): lax.all_gather(left_factor, 'tok', axis=0, tiled=True)  22.3 us
    another operation x9, other arithmetic, orthonormal(): lower_factor = jnp.linalg.cholesky(gram_matrix)  10.8 us
    all_to_all x1, blocking collectives, per_device(): lax.all_to_all(attended, 'tok', split_axis=0, concat_axis=0, tiled=True)  10.5 us
    another operation x6, other arithmetic, orthonormal(): jax.scipy.linalg.solve_triangular(lower_factor, block_cols.T, lower=True)  9.26 us
    all_to_all x1, starting transfers between devices, per_device(): lax.all_to_all(q_blocks, 'tok', split_axis=0, concat_axis=0, tiled=True)  7.39 us
    all_to_all x1, starting transfers between devices, per_device(): lax.all_to_all(w_blocks, 'tok', split_axis=0, concat_axis=0, tiled=True)  6.01 us
    dot_general x1, matrix products, per_device(): jnp.dot(row_block, w_out, preferred_element_type=jnp.float32)  4.56 us
    dot_general x2, matrix products, compress(): basis_cols = orthonormal(jnp.dot(delta_block, inner, precision=highest))  2.69 us
  transfers between devices with their start and end apart: 2, of which 0 were waited for; matrix products, arithmetic and copies ran while one was open for 33% of the time, Pallas kernels for 0%

commit v1 on v0

v1 whole, which is shorter than its diff:
```python
import functools
import math

import jax
import jax.numpy as jnp
from jax import lax
from jax.experimental import pallas as pl
from jax.experimental.pallas import tpu as pltpu
from jax.sharding import PartitionSpec as P

HD = 64
SWEEPS = 2
LANES = 128
NT = (((1,), (1,)), ((), ()))
NN = (((1,), (0,)), ((), ()))
highest = lax.Precision.HIGHEST
f32 = jnp.float32
bf16 = jnp.bfloat16


def up(value, to):
    return -(-value // to) * to


def matmul(a, b, dims, precision=None):
    return lax.dot_general(a, b, dims, precision=precision, preferred_element_type=f32)


def split(x):
    high = x.astype(bf16)
    return high, (x - high.astype(f32)).astype(bf16)


def eliminate(m, cols, width):
    rank = m.shape[0]
    row_id = lax.broadcasted_iota(jnp.int32, m.shape, 0)
    scale = jnp.zeros_like(m)
    for start in range(0, rank, width):
        col = [jnp.broadcast_to(m[:, cols + start + k : cols + start + k + 1], m.shape) for k in range(width)]
        row = [jnp.broadcast_to(m[start + k : start + k + 1, :], (8, m.shape[1])) for k in range(width)]
        cell = [
            [jnp.broadcast_to(col[b][start + a : start + a + 1, :], (8, m.shape[1])) for b in range(a + 1)]
            for a in range(width)
        ]
        for k in range(width):
            inverse = 1.0 / cell[k][k]
            times = {a: cell[a][k] * inverse for a in range(k + 1, width)}
            tall = lambda x: jnp.concatenate([x] * (rank // 8), axis=0)
            below = jnp.where(row_id > start + k, col[k], 0.0) * tall(inverse)
            m = m - below * tall(row[k])
            scale = jnp.where(row_id == start + k, tall(cell[k][k]), scale)
            for a in range(k + 1, width):
                for b in range(k + 1, a + 1):
                    cell[a][b] = cell[a][b] - times[a] * cell[b][k]
                row[a] = row[a] - times[a] * row[k]
                col[a] = col[a] - tall(times[a]) * col[k]
    return m * lax.rsqrt(scale)


def compress_kernel(
    plan,
    base_ref,
    live_ref,
    new_ref,
    prev_ref,
    sketch_ref,
    q_ref,
    cache_ref,
    w_ref,
    out_ref,
    limits_ref,
    cache_out,
    w_out,
    new_buf,
    prev_buf,
    sketch_buf,
    q_buf,
    live_buf,
    terms,
    new_sems,
    prev_sems,
    sketch_sems,
    sems,
):
    tokens, columns = new_ref.shape
    rank = sketch_ref.shape[0]
    chunks = new_buf.shape[0]
    step = columns // chunks
    gap = up(tokens, LANES)
    per_dev, parts, part_rows, q_at, left_at = plan
    receivers = out_ref.shape[0]
    groups = receivers // parts
    base = jnp.where(base_ref[0] == 1, 1, 0)
    copies = []
    for c in range(chunks):
        at = pl.ds(c * step, step)
        trio = (
            pltpu.make_async_copy(new_ref.at[:, at], new_buf.at[c], new_sems.at[c]),
            pltpu.make_async_copy(prev_ref.at[base, :, at], prev_buf.at[c], prev_sems.at[c]),
            pltpu.make_async_copy(sketch_ref.at[:, at], sketch_buf.at[c], sketch_sems.at[c]),
        )
        for copy in trio:
            copy.start()
        copies.append(trio)
    q_copy = pltpu.make_async_copy(q_ref, q_buf, sems.at[0])
    live_copy = pltpu.make_async_copy(live_ref, live_buf, sems.at[1])
    later = (
        pltpu.make_async_copy(cache_ref, cache_out, sems.at[2]),
        pltpu.make_async_copy(w_ref, w_out, sems.at[3]),
    )
    for copy in (q_copy, live_copy) + later:
        copy.start()

    if gap > tokens:
        terms[tokens:gap, :] = jnp.zeros((gap - tokens, columns), bf16)
    total = jnp.zeros((tokens + 2 * rank, gap + tokens), f32)
    for c in range(chunks):
        at = slice(c * step, (c + 1) * step)
        for copy in copies[c]:
            copy.wait()
        delta = new_buf[c].astype(f32) - prev_buf[c].astype(f32)
        high, low = split(delta)
        terms[0:tokens, at] = high
        terms[gap : gap + tokens, at] = low
        s_high, s_low = split(sketch_buf[c])
        total = total + matmul(jnp.concatenate([high, s_high, s_low], axis=0), terms[:, at], NT)
    q_copy.wait()
    for g in range(groups):
        for j in range(parts):
            if q_buf.ndim == 2:
                block = q_buf[j * part_rows : (j + 1) * part_rows, g * LANES : (g + 1) * LANES]
            else:
                block = q_buf[g * parts + j]
            out_ref[g * parts + j, q_at : q_at + block.shape[0], :] = block

    live_copy.wait()
    for s in range(receivers):
        limits_ref[s : s + 1, :] = jnp.full((1, LANES), live_buf[s], jnp.int32)

    cross = total[:tokens, gap:]
    gram = total[:tokens, :tokens] + cross + cross.T
    sketched = total[tokens : tokens + rank]
    y = sketched[:, :tokens] + sketched[:, gap:] + total[tokens + rank :, :tokens]

    eye = jnp.where(
        lax.broadcasted_iota(jnp.int32, (tokens, tokens), 0) == lax.broadcasted_iota(jnp.int32, (tokens, tokens), 1),
        1.0,
        0.0,
    )
    for sweep in range(SWEEPS + 1):
        if sweep:
            y = matmul(basis, gram, NN, highest)
        both = matmul(y, jnp.concatenate([eye, y], axis=0), NT, highest)
        basis = eliminate(both, tokens, 4)[:, :tokens]

    high, low = split(basis)
    blank = jnp.zeros((rank, gap - tokens), bf16)
    first = jnp.concatenate([high, blank, high] if gap > tokens else [high, high], axis=1)
    second = jnp.concatenate([low, jnp.zeros((rank, gap), bf16)], axis=1)
    lhs = jnp.concatenate([first, second], axis=0)

    blocks = LANES // rank
    packed_rows = tokens // blocks
    tiled = jnp.concatenate([high] * blocks, axis=0)
    lane = lax.broadcasted_iota(jnp.int32, (packed_rows, LANES), 1)
    packed = jnp.zeros((packed_rows, LANES), f32)
    for k in range(blocks):
        pick = (
            lax.broadcasted_iota(jnp.int32, (packed_rows, tokens), 1)
            == lax.broadcasted_iota(jnp.int32, (packed_rows, tokens), 0) + k * packed_rows
        )
        packed = jnp.where(lane // rank == k, matmul(jnp.where(pick, 1.0, 0.0).astype(bf16), tiled, NT), packed)
    packed = packed.astype(bf16)

    width = 2 * HD
    for g in range(groups):
        for d in range(per_dev):
            head = g * per_dev + d
            pair = matmul(lhs, terms[:, head * width : (head + 1) * width], NN)
            block = (pair[:rank] + pair[rank:]).astype(bf16)
            for j in range(parts):
                out_ref[g * parts + j, d * rank : (d + 1) * rank, :] = block
        for j in range(parts):
            out_ref[g * parts + j, left_at : left_at + packed_rows, :] = packed
    for copy in later:
        copy.wait()


def attend_kernel(plan, block_rows, limits_ref, got_ref, cache_ref, out_ref, keys, values, q_all):
    per_dev, part_rows, rank, tokens, q_at, left_at = plan
    shards = got_ref.shape[0]
    blocks = LANES // rank
    packed_rows = tokens // blocks
    lane_p = lax.broadcasted_iota(jnp.int32, (packed_rows, LANES), 1)
    lane_t = lax.broadcasted_iota(jnp.int32, (tokens, LANES), 1)
    row_t = lax.broadcasted_iota(jnp.int32, (tokens, LANES), 0)

    def one_shard(s, carry):
        packed = got_ref[s, left_at : left_at + packed_rows, :].astype(f32)
        left = jnp.concatenate([jnp.where(lane_p // rank == k, packed, 0.0) for k in range(blocks)], axis=0).astype(bf16)
        at = pl.ds(pl.multiple_of(s * tokens, tokens), tokens)
        dead = jnp.where((lane_t == HD) & (row_t >= limits_ref[pl.ds(s, 1), :]), -1e30, 0.0)
        right = jnp.concatenate([got_ref[s, d * rank : (d + 1) * rank, :] for d in range(per_dev)], axis=1)
        lowrank = matmul(left, jnp.concatenate([right] * blocks, axis=0), NN).astype(bf16)
        for d in range(per_dev):
            both = cache_ref[d, at, :].astype(f32) + lowrank[:, d * LANES : (d + 1) * LANES].astype(f32)
            keys[d, at, :] = jnp.where(lane_t < HD, both, dead).astype(bf16)
            values[d, at, :] = jnp.where(lane_t < HD, 1.0, both).astype(bf16)
        return carry

    lax.fori_loop(0, shards, one_shard, 0, unroll=math.gcd(shards, 16))

    padded = got_ref[:, q_at : q_at + up(part_rows, 16), :].astype(f32)
    q_rows = padded[:, :part_rows, :].reshape(shards * part_rows, LANES)
    lane_q = lax.broadcasted_iota(jnp.int32, q_rows.shape, 1)
    for d in range(per_dev):
        moved = q_rows if d == 0 else pltpu.roll(q_rows, LANES - d * HD, 1)
        q_all[d] = jnp.where(lane_q < HD, moved * HD**-0.5, jnp.where(lane_q == HD, 1.0, 0.0)).astype(bf16)

    lane_o = lax.broadcasted_iota(jnp.int32, (block_rows, LANES), 1)

    def one_block(b, carry):
        at = pl.ds(pl.multiple_of(b * block_rows, block_rows), block_rows)
        out = jnp.zeros((block_rows, LANES), f32)
        for d in range(per_dev):
            scores = matmul(q_all[d, at, :], keys[d], NT)
            exponent = jnp.exp(scores - jnp.max(scores, axis=1, keepdims=True)).astype(bf16)
            sums = matmul(exponent, values[d], NN)
            flipped = pltpu.roll(sums, HD, 1)
            if d == 0:
                out = flipped / sums
            else:
                out = jnp.where(lane_o < HD, out, sums / flipped)
        out_ref[at, :] = out.astype(bf16)
        return carry

    count = shards * part_rows // block_rows
    if count == 1:
        one_block(0, 0)
    else:
        lax.fori_loop(0, count, one_block, 0)


def project_kernel(x_ref, w_ref, out_ref, buf, sems):
    chunks, rows, step = buf.shape
    copies = []
    for c in range(chunks):
        at = slice(c * step, (c + 1) * step)
        buf[c] = matmul(x_ref[...], w_ref[:, at], NN).astype(bf16)
        copies.append(pltpu.make_async_copy(buf.at[c], out_ref.at[:, pl.ds(c * step, step)], sems.at[c]))
        copies[c].start()
    for copy in copies:
        copy.wait()


def per_device(queries, new_kv, prev_kv, base_step, live_counts, sketch, cache, w_out):
    shards = lax.axis_size("tok")
    tokens, columns = new_kv.shape
    rank = sketch.shape[1]
    query_rows = queries.shape[0]
    head_count = queries.shape[1] // HD
    parts = max(1, shards // head_count)
    per_dev = head_count * parts // shards
    groups = head_count // per_dev
    part_rows = query_rows // parts
    key_count = shards * tokens
    query_count = shards * part_rows
    q_width = per_dev * HD

    q_at = per_dev * rank
    left_at = q_at + up(part_rows, 16)
    rows = left_at + tokens * rank // LANES
    if q_width == LANES and part_rows % 16 == 0:
        q_in = queries
    else:
        q_in = queries.reshape(parts, part_rows, groups, q_width).transpose(2, 0, 1, 3)
        q_in = q_in.reshape(shards, part_rows, q_width)
        q_in = jnp.pad(q_in, ((0, 0), (0, up(part_rows, 16) - part_rows), (0, LANES - q_width)))

    vmem = pl.BlockSpec(memory_space=pltpu.VMEM)
    smem = pl.BlockSpec(memory_space=pltpu.SMEM)
    chunks = 4
    step = columns // chunks
    hbm = pl.BlockSpec(memory_space=pltpu.HBM)
    inputs = (live_counts, new_kv, prev_kv, sketch.T, q_in, cache, w_out)
    inputs = [pltpu.with_memory_space_constraint(x, pltpu.HBM) for x in inputs]
    send, limits, cache, w_out = pl.pallas_call(
        functools.partial(compress_kernel, (per_dev, parts, part_rows, q_at, left_at)),
        out_shape=(
            jax.ShapeDtypeStruct((shards, rows, LANES), bf16),
            jax.ShapeDtypeStruct((shards, LANES), jnp.int32),
            jax.ShapeDtypeStruct(cache.shape, bf16),
            jax.ShapeDtypeStruct(w_out.shape, bf16),
        ),
        in_specs=[smem] + [hbm] * 7,
        out_specs=(vmem,) * 4,
        scratch_shapes=[
            pltpu.VMEM((chunks, tokens, step), bf16),
            pltpu.VMEM((chunks, tokens, step), bf16),
            pltpu.VMEM((chunks, rank, step), f32),
            pltpu.VMEM(q_in.shape, bf16),
            pltpu.SMEM((shards,), jnp.int32),
            pltpu.VMEM((up(tokens, LANES) + tokens, columns), bf16),
            pltpu.SemaphoreType.DMA((chunks,)),
            pltpu.SemaphoreType.DMA((chunks,)),
            pltpu.SemaphoreType.DMA((chunks,)),
            pltpu.SemaphoreType.DMA((4,)),
        ],
        compiler_params=pltpu.CompilerParams(vmem_limit_bytes=20 << 20),
        name="compress",
    )(base_step, *inputs)

    got = lax.all_to_all(send, "tok", split_axis=0, concat_axis=0, tiled=True)

    block_rows = query_count
    while block_rows * key_count * 4 > (4 << 20):
        block_rows //= 2
    attended = pl.pallas_call(
        functools.partial(attend_kernel, (per_dev, part_rows, rank, tokens, q_at, left_at), block_rows),
        out_shape=jax.ShapeDtypeStruct((query_count, LANES), bf16),
        in_specs=[vmem, vmem, vmem],
        out_specs=vmem,
        scratch_shapes=[
            pltpu.VMEM((per_dev, key_count, LANES), bf16),
            pltpu.VMEM((per_dev, key_count, LANES), bf16),
            pltpu.VMEM((per_dev, query_count, LANES), bf16),
        ],
        compiler_params=pltpu.CompilerParams(vmem_limit_bytes=32 << 20),
        name="attend",
    )(limits, got, cache)
    attended = attended.reshape(shards, part_rows, LANES)[:, :, :q_width]

    returned = lax.all_to_all(attended, "tok", split_axis=0, concat_axis=0, tiled=True)
    returned = returned.reshape(groups, parts, part_rows, q_width)
    row_block = returned.transpose(1, 2, 0, 3).reshape(query_rows, head_count * HD)
    chunks = 2
    return pl.pallas_call(
        project_kernel,
        out_shape=jax.ShapeDtypeStruct((query_rows, w_out.shape[1]), bf16),
        in_specs=[vmem, vmem],
        out_specs=hbm,
        scratch_shapes=[
            pltpu.VMEM((chunks, query_rows, w_out.shape[1] // chunks), bf16),
            pltpu.SemaphoreType.DMA((chunks,)),
        ],
        compiler_params=pltpu.CompilerParams(vmem_limit_bytes=8 << 20),
        name="project",
    )(row_block, w_out)


def solution(mesh):
    return jax.shard_map(
        per_device,
        mesh=mesh,
        in_specs=(
            P(("groups", "tok"), None),
            P(("groups", "tok"), None),
            P(None, ("groups", "tok"), None),
            P(("groups", "tok")),
            P("groups"),
            P(),
            P(("groups", "tok"), None, None),
            P(),
        ),
        out_specs=P(("groups", "tok"), None),
        check_vma=False,
    )
```

time: 95.2 us -> 47.5 us (0.50)
  other arithmetic: 24.6 us -> 0 us
  matrix products: 17.5 us -> 0 us
  Pallas kernels: 0 us -> 13.9 us
  starting transfers between devices: 13.4 us -> 0 us
  local copies, waits for them, and re-layouts: 5.45 us -> 0.09 us
    all_gather x1 -> x0, blocking collectives: 22.3 us -> none  [per_device(): lax.all_gather(left_factor, 'tok', axis=0, tiled=True)]
    all_to_all x0 -> x1, blocking collectives: none -> 20.9 us  [per_device(): got = lax.all_to_all(send, 'tok', split_axis=0, concat_axis=0, tiled=True)]
    another operation x15 -> x0, other arithmetic: 20.1 us -> none  [the longest x9 10.8 us: orthonormal(): lower_factor = jnp.linalg.cholesky(gram_matrix)]
    dot_general x15 -> x0, matrix products: 16.8 us -> none  [the longest x1 4.56 us: per_device(): jnp.dot(row_block, w_out, preferred_element_type=jnp.float32)]
    pallas_call x0 -> x3, Pallas kernels: none -> 13.9 us  [the longest x1 8.82 us: per_device(): pl.pallas_call(functools.partial(compress_kernel, (per_dev, parts, part_r...]
    all_to_all x2 -> x0, starting transfers between devices: 13.4 us -> none  [the longest x1 7.39 us: per_device(): lax.all_to_all(q_blocks, 'tok', split_axis=0, concat_axis=0, tiled=True)]
    convert_element_type x1 -> x0, local copies, waits for them, and re-layouts: 2.05 us -> none  [per_device(): lowrank.astype(jnp.float32)]
    sub x1 -> x0, other arithmetic: 1.88 us -> none  [per_device(): delta = new_kv.astype(jnp.float32) - prior]
  transfers between devices with their start and end apart: 2 -> 0, of which waited for: 0 -> 0; matrix products, arithmetic and copies ran while one was open for 33% -> 0% of each run, Pallas kernels for 0% -> 0%
where the time goes in v1:
time: 47.5 us; the launch traced here: 47.3 us
  blocking collectives  32.6 us (69%)
  Pallas kernels  13.9 us (29%)
  between operations  0.68 us (1%)
    all_to_all x1, blocking collectives, per_device(): got = lax.all_to_all(send, 'tok', split_axis=0, concat_axis=0, tiled=True)  20.9 us
    all_to_all x1, blocking collectives, per_device(): lax.all_to_all(attended, 'tok', split_axis=0, concat_axis=0, tiled=True)  11.7 us
    pallas_call x1, Pallas kernels, per_device(): pl.pallas_call(functools.partial(compress_kernel, (per_dev, parts, part_r...  8.82 us
    pallas_call x1, Pallas kernels, per_device(): pl.pallas_call(functools.partial(attend_kernel, (per_dev, part_rows, rank...  3.22 us
    pallas_call x1, Pallas kernels, per_device(): pl.pallas_call(project_kernel, out_shape=jax.ShapeDtypeStruct((query_rows...  1.82 us

profile of v1, /device:TPU:0, one launch (start us, length us, event | category | flops | bytes accessed | tf_op | source)
XLA Modules:
  0.0 47.3 jit_solution(796852862440858090)
XLA Ops:
  0.7 8.8 %compress.1 = (bf16[16,120,128]{2,1,0:T(8,128)(2,1)S(1)}, s32[16,128]{1,0:T(8,128)S(1)}, bf16[2,1536,128]{2,1,0:T(8,128)(2,1)S(1)}, bf16[2048,1536]{1,0:T(8,128)(2,1)S(1)}) custom-call(s32[1]{0:T(128)S(6)} %copy.14.base_ref, s32[16]{0:T(128)} %live_ref.1, bf16[96,4096]{1,0:T(8,128)(2,1)} %new_ref.1, bf16[2,96,4096]{2,1,0:T(8,128)(2,1)} %prev_ref.1, ...), custom_call_target="tpu_custom_call" | custom-call | tf_op jit(solution)/shard_map/compress/pallas_call | solution.py:287
  9.5 20.9 %all_to_all.10.got_ref = bf16[16,120,128]{2,1,0:T(8,128)(2,1)S(1)} all-to-all(bf16[16,120,128]{2,1,0:T(8,128)(2,1)S(1)} %get-tuple-element.10), channel_id=1, replica_groups=mesh['groups'=2,'tok'=16] {'tok'}, dimensions={0} | all-to-all | bytes 983040 | tf_op jit(solution)/shard_map/all_to_all | solution.py:313
  30.4 3.2 %attend.1 = bf16[512,128]{1,0:T(8,128)(2,1)S(1)} custom-call(s32[16,128]{1,0:T(8,128)S(1)} %get-tuple-element.9.limits_ref, bf16[16,120,128]{2,1,0:T(8,128)(2,1)S(1)} %all_to_all.10.got_ref, bf16[2,1536,128]{2,1,0:T(8,128)(2,1)S(1)} %get-tuple-element.11.cache_ref), custom_call_target="tpu_custom_call" | custom-call | tf_op jit(solution)/shard_map/attend/pallas_call | solution.py:318
  33.6 11.7 %all_to_all.11 = bf16[16,32,128]{2,1,0:T(8,128)(2,1)S(1)} all-to-all(bf16[16,32,128]{2,1,0:T(8,128)(2,1)S(1)} %bitcast.11), channel_id=1, replica_groups=mesh['groups'=2,'tok'=16] {'tok'}, dimensions={0} | all-to-all | bytes 262144 | tf_op jit(solution)/shard_map/all_to_all | solution.py:333
  45.3 0.1 copy.10
  45.4 1.8 %project.1 = bf16[32,1536]{1,0:T(8,128)(2,1)} custom-call(bf16[32,2048]{1,0:T(8,128)(2,1)S(1)} %bitcast.10, bf16[2048,1536]{1,0:T(8,128)(2,1)S(1)} %get-tuple-element.12.w_ref), custom_call_target="tpu_custom_call" | custom-call | tf_op jit(solution)/shard_map/project/pallas_call | solution.py:337
  (1 shorter events, 0.0 us)

commit v2 on v1

--- a/solution.py
+++ b/solution.py
@@ -31,30 +31,38 @@
     return high, (x - high.astype(f32)).astype(bf16)
 
 
-def eliminate(m, cols, width):
-    rank = m.shape[0]
-    row_id = lax.broadcasted_iota(jnp.int32, m.shape, 0)
-    scale = jnp.zeros_like(m)
-    for start in range(0, rank, width):
-        col = [jnp.broadcast_to(m[:, cols + start + k : cols + start + k + 1], m.shape) for k in range(width)]
-        row = [jnp.broadcast_to(m[start + k : start + k + 1, :], (8, m.shape[1])) for k in range(width)]
-        cell = [
-            [jnp.broadcast_to(col[b][start + a : start + a + 1, :], (8, m.shape[1])) for b in range(a + 1)]
-            for a in range(width)
-        ]
-        for k in range(width):
-            inverse = 1.0 / cell[k][k]
-            times = {a: cell[a][k] * inverse for a in range(k + 1, width)}
-            tall = lambda x: jnp.concatenate([x] * (rank // 8), axis=0)
-            below = jnp.where(row_id > start + k, col[k], 0.0) * tall(inverse)
-            m = m - below * tall(row[k])
-            scale = jnp.where(row_id == start + k, tall(cell[k][k]), scale)
-            for a in range(k + 1, width):
-                for b in range(k + 1, a + 1):
-                    cell[a][b] = cell[a][b] - times[a] * cell[b][k]
+def eliminate(m, cols):
+    rank, wide = m.shape
+    tile = 8
+    rest = [m[i : i + tile] for i in range(0, rank, tile)]
+    row_id = lax.broadcasted_iota(jnp.int32, (tile, wide), 0)
+    spread = lambda x, i: jnp.broadcast_to(x[i : i + 1], (tile, wide))
+    done = []
+    for start in range(0, rank, tile):
+        lane = [jnp.full((tile, wide), cols + start + k, jnp.int32) for k in range(tile)]
+        col = [[jnp.take_along_axis(r, at, axis=1, mode="promise_in_bounds") for r in rest] for at in lane]
+        row = [spread(rest[0], k) for k in range(tile)]
+        head = jnp.zeros((tile, wide), f32)
+        pivot = spread(col[0][0], 0)
+        for k in range(tile):
+            later = range(k + 1, tile)
+            ahead = {a: spread(col[a][0], k) for a in later}
+            following = spread(col[k + 1][0], k + 1) if k + 1 < tile else None
+            root = lax.rsqrt(pivot)
+            times = {a: ahead[a] * root for a in later}
+            if k + 1 < tile:
+                pivot = following - times[k + 1] * times[k + 1]
+            row[k] = row[k] * root
+            head = jnp.where(row_id == k, row[k], head)
+            below = [c * root for c in col[k]]
+            for a in later:
                 row[a] = row[a] - times[a] * row[k]
-                col[a] = col[a] - tall(times[a]) * col[k]
-    return m * lax.rsqrt(scale)
+                col[a] = [c - times[a] * d for c, d in zip(col[a], below)]
+            for i in range(1, len(rest)):
+                rest[i] = rest[i] - below[i] * row[k]
+        done.append(head)
+        rest = rest[1:]
+    return jnp.concatenate(done, axis=0)
 
 
 def compress_kernel(
@@ -68,7 +76,7 @@
     cache_ref,
     w_ref,
     out_ref,
-    limits_ref,
+    dead_ref,
     cache_out,
     w_out,
     new_buf,
@@ -86,11 +94,14 @@
     rank = sketch_ref.shape[0]
     chunks = new_buf.shape[0]
     step = columns // chunks
-    gap = up(tokens, LANES)
     per_dev, parts, part_rows, q_at, left_at = plan
     receivers = out_ref.shape[0]
     groups = receivers // parts
     base = jnp.where(base_ref[0] == 1, 1, 0)
+    q_copy = pltpu.make_async_copy(q_ref, q_buf, sems.at[0])
+    live_copy = pltpu.make_async_copy(live_ref, live_buf, sems.at[1])
+    live_copy.start()
+    q_copy.start()
     copies = []
     for c in range(chunks):
         at = pl.ds(c * step, step)
@@ -102,28 +113,19 @@
         for copy in trio:
             copy.start()
         copies.append(trio)
-    q_copy = pltpu.make_async_copy(q_ref, q_buf, sems.at[0])
-    live_copy = pltpu.make_async_copy(live_ref, live_buf, sems.at[1])
     later = (
         pltpu.make_async_copy(cache_ref, cache_out, sems.at[2]),
         pltpu.make_async_copy(w_ref, w_out, sems.at[3]),
     )
-    for copy in (q_copy, live_copy) + later:
+    for copy in later:
         copy.start()
 
-    if gap > tokens:
-        terms[tokens:gap, :] = jnp.zeros((gap - tokens, columns), bf16)
-    total = jnp.zeros((tokens + 2 * rank, gap + tokens), f32)
-    for c in range(chunks):
-        at = slice(c * step, (c + 1) * step)
-        for copy in copies[c]:
-            copy.wait()
-        delta = new_buf[c].astype(f32) - prev_buf[c].astype(f32)
-        high, low = split(delta)
-        terms[0:tokens, at] = high
-        terms[gap : gap + tokens, at] = low
-        s_high, s_low = split(sketch_buf[c])
-        total = total + matmul(jnp.concatenate([high, s_high, s_low], axis=0), terms[:, at], NT)
+    live_copy.wait()
+    row_t = lax.broadcasted_iota(jnp.int32, (tokens, LANES), 0)
+    lane_t = lax.broadcasted_iota(jnp.int32, (tokens, LANES), 1)
+    edge = jnp.where(lane_t == HD, row_t, -1)
+    for s in range(receivers):
+        dead_ref[s] = jnp.where(edge >= live_buf[s], -1e30, 0.0).astype(bf16)
     q_copy.wait()
     for g in range(groups):
         for j in range(parts):
@@ -131,16 +133,25 @@
                 block = q_buf[j * part_rows : (j + 1) * part_rows, g * LANES : (g + 1) * LANES]
             else:
                 block = q_buf[g * parts + j]
-            out_ref[g * parts + j, q_at : q_at + block.shape[0], :] = block
-
-    live_copy.wait()
-    for s in range(receivers):
-        limits_ref[s : s + 1, :] = jnp.full((1, LANES), live_buf[s], jnp.int32)
-
-    cross = total[:tokens, gap:]
-    gram = total[:tokens, :tokens] + cross + cross.T
-    sketched = total[tokens : tokens + rank]
-    y = sketched[:, :tokens] + sketched[:, gap:] + total[tokens + rank :, :tokens]
+            out_ref[g * parts + j, q_at : q_at + block.shape[0], :] = block * bf16(HD**-0.5)
+
+    both_sums = [jnp.zeros((tokens + 2 * rank, 2 * tokens), f32)] * 2
+    for c in range(chunks):
+        at = slice(c * step, (c + 1) * step)
+        for copy in copies[c]:
+            copy.wait()
+        delta = new_buf[c].astype(f32) - prev_buf[c].astype(f32)
+        high, low = split(delta)
+        terms[:, at] = high
+        s_high, s_low = split(sketch_buf[c])
+        lhs = jnp.concatenate([high, s_high, s_low], axis=0)
+        rhs = jnp.concatenate([high, low], axis=0)
+        for k in range(0, step, 256):
+            both_sums[(k // 256) % 2] = both_sums[(k // 256) % 2] + matmul(lhs[:, k : k + 256], rhs[:, k : k + 256], NT)
+    sums = both_sums[0] + both_sums[1]
+    total, cross = sums[:, :tokens], sums[:, tokens:]
+    gram = total[:tokens] + cross[:tokens] + cross[:tokens].T
+    y = total[tokens : tokens + rank] + total[tokens + rank :] + cross[tokens : tokens + rank]
 
     eye = jnp.where(
         lax.broadcasted_iota(jnp.int32, (tokens, tokens), 0) == lax.broadcasted_iota(jnp.int32, (tokens, tokens), 1),
@@ -151,13 +162,10 @@
         if sweep:
             y = matmul(basis, gram, NN, highest)
         both = matmul(y, jnp.concatenate([eye, y], axis=0), NT, highest)
-        basis = eliminate(both, tokens, 4)[:, :tokens]
+        basis = eliminate(both, tokens)[:, :tokens]
 
     high, low = split(basis)
-    blank = jnp.zeros((rank, gap - tokens), bf16)
-    first = jnp.concatenate([high, blank, high] if gap > tokens else [high, high], axis=1)
-    second = jnp.concatenate([low, jnp.zeros((rank, gap), bf16)], axis=1)
-    lhs = jnp.concatenate([first, second], axis=0)
+    lhs = jnp.concatenate([high, low], axis=0)
 
     blocks = LANES // rank
     packed_rows = tokens // blocks
@@ -172,40 +180,37 @@
         packed = jnp.where(lane // rank == k, matmul(jnp.where(pick, 1.0, 0.0).astype(bf16), tiled, NT), packed)
     packed = packed.astype(bf16)
 
-    width = 2 * HD
+    width = 2 * HD * per_dev
     for g in range(groups):
-        for d in range(per_dev):
-            head = g * per_dev + d
-            pair = matmul(lhs, terms[:, head * width : (head + 1) * width], NN)
-            block = (pair[:rank] + pair[rank:]).astype(bf16)
-            for j in range(parts):
-                out_ref[g * parts + j, d * rank : (d + 1) * rank, :] = block
+        pair = matmul(lhs, terms[:, g * width : (g + 1) * width], NN)
+        block = (pair[:rank] + pair[rank:]).astype(bf16)
         for j in range(parts):
+            for d in range(per_dev):
+                out_ref[g * parts + j, d * rank : (d + 1) * rank, :] = block[:, d * LANES : (d + 1) * LANES]
             out_ref[g * parts + j, left_at : left_at + packed_rows, :] = packed
     for copy in later:
         copy.wait()
 
 
-def attend_kernel(plan, block_rows, limits_ref, got_ref, cache_ref, out_ref, keys, values, q_all):
+def attend_kernel(plan, block_rows, dead_ref, got_ref, cache_ref, out_ref, keys, values, q_all):
     per_dev, part_rows, rank, tokens, q_at, left_at = plan
     shards = got_ref.shape[0]
     blocks = LANES // rank
     packed_rows = tokens // blocks
     lane_p = lax.broadcasted_iota(jnp.int32, (packed_rows, LANES), 1)
-    lane_t = lax.broadcasted_iota(jnp.int32, (tokens, LANES), 1)
-    row_t = lax.broadcasted_iota(jnp.int32, (tokens, LANES), 0)
+    is_key = lax.broadcasted_iota(jnp.int32, (tokens, LANES), 1) < HD
+    ones = jnp.ones((tokens, LANES), bf16)
 
     def one_shard(s, carry):
         packed = got_ref[s, left_at : left_at + packed_rows, :].astype(f32)
         left = jnp.concatenate([jnp.where(lane_p // rank == k, packed, 0.0) for k in range(blocks)], axis=0).astype(bf16)
         at = pl.ds(pl.multiple_of(s * tokens, tokens), tokens)
-        dead = jnp.where((lane_t == HD) & (row_t >= limits_ref[pl.ds(s, 1), :]), -1e30, 0.0)
         right = jnp.concatenate([got_ref[s, d * rank : (d + 1) * rank, :] for d in range(per_dev)], axis=1)
         lowrank = matmul(left, jnp.concatenate([right] * blocks, axis=0), NN).astype(bf16)
         for d in range(per_dev):
-            both = cache_ref[d, at, :].astype(f32) + lowrank[:, d * LANES : (d + 1) * LANES].astype(f32)
-            keys[d, at, :] = jnp.where(lane_t < HD, both, dead).astype(bf16)
-            values[d, at, :] = jnp.where(lane_t < HD, 1.0, both).astype(bf16)
+            both = cache_ref[d, at, :] + lowrank[:, d * LANES : (d + 1) * LANES]
+            keys[d, at, :] = jnp.where(is_key, both, dead_ref[s])
+            values[d, at, :] = jnp.where(is_key, ones, both)
         return carry
 
     lax.fori_loop(0, shards, one_shard, 0, unroll=math.gcd(shards, 16))
@@ -215,7 +220,7 @@
     lane_q = lax.broadcasted_iota(jnp.int32, q_rows.shape, 1)
     for d in range(per_dev):
         moved = q_rows if d == 0 else pltpu.roll(q_rows, LANES - d * HD, 1)
-        q_all[d] = jnp.where(lane_q < HD, moved * HD**-0.5, jnp.where(lane_q == HD, 1.0, 0.0)).astype(bf16)
+        q_all[d] = jnp.where(lane_q < HD, moved, jnp.where(lane_q == HD, 1.0, 0.0)).astype(bf16)
 
     lane_o = lax.broadcasted_iota(jnp.int32, (block_rows, LANES), 1)
 
@@ -284,11 +289,11 @@
     hbm = pl.BlockSpec(memory_space=pltpu.HBM)
     inputs = (live_counts, new_kv, prev_kv, sketch.T, q_in, cache, w_out)
     inputs = [pltpu.with_memory_space_constraint(x, pltpu.HBM) for x in inputs]
-    send, limits, cache, w_out = pl.pallas_call(
+    send, dead, cache, w_out = pl.pallas_call(
         functools.partial(compress_kernel, (per_dev, parts, part_rows, q_at, left_at)),
         out_shape=(
             jax.ShapeDtypeStruct((shards, rows, LANES), bf16),
-            jax.ShapeDtypeStruct((shards, LANES), jnp.int32),
+            jax.ShapeDtypeStruct((shards, tokens, LANES), bf16),
             jax.ShapeDtypeStruct(cache.shape, bf16),
             jax.ShapeDtypeStruct(w_out.shape, bf16),
         ),
@@ -300,7 +305,7 @@
             pltpu.VMEM((chunks, rank, step), f32),
             pltpu.VMEM(q_in.shape, bf16),
             pltpu.SMEM((shards,), jnp.int32),
-            pltpu.VMEM((up(tokens, LANES) + tokens, columns), bf16),
+            pltpu.VMEM((tokens, columns), bf16),
             pltpu.SemaphoreType.DMA((chunks,)),
             pltpu.SemaphoreType.DMA((chunks,)),
             pltpu.SemaphoreType.DMA((chunks,)),
@@ -327,7 +332,7 @@
         ],
         compiler_params=pltpu.CompilerParams(vmem_limit_bytes=32 << 20),
         name="attend",
-    )(limits, got, cache)
+    )(dead, got, cache)
     attended = attended.reshape(shards, part_rows, LANES)[:, :, :q_width]
 
     returned = lax.all_to_all(attended, "tok", split_axis=0, concat_axis=0, tiled=True)

time: 47.5 us -> 44.9 us (0.945)
  Pallas kernels: 13.9 us -> 11.3 us
    pallas_call x1, Pallas kernels: 8.82 us -> 6.38 us  [per_device(): pl.pallas_call(functools.partial(compress_kernel, (per_dev, parts, part_r...]
where the time goes in v2:
time: 44.9 us; the launch traced here: 44.7 us
  blocking collectives  32.6 us (73%)
  Pallas kernels  11.3 us (25%)
  between operations  0.68 us (2%)
    all_to_all x1, blocking collectives, per_device(): got = lax.all_to_all(send, 'tok', split_axis=0, concat_axis=0, tiled=True)  20.9 us
    all_to_all x1, blocking collectives, per_device(): lax.all_to_all(attended, 'tok', split_axis=0, concat_axis=0, tiled=True)  11.7 us
    pallas_call x1, Pallas kernels, per_device(): pl.pallas_call(functools.partial(compress_kernel, (per_dev, parts, part_r...  6.38 us
    pallas_call x1, Pallas kernels, per_device(): pl.pallas_call(functools.partial(attend_kernel, (per_dev, part_rows, rank...  3.12 us
    pallas_call x1, Pallas kernels, per_device(): pl.pallas_call(project_kernel, out_shape=jax.ShapeDtypeStruct((query_rows...  1.82 us

profile of v2, /device:TPU:0, one launch (start us, length us, event | category | flops | bytes accessed | tf_op | source)
XLA Modules:
  0.0 44.7 jit_solution(219164767007284097)
XLA Ops:
  0.7 6.4 %compress.1 = (bf16[16,120,128]{2,1,0:T(8,128)(2,1)S(1)}, bf16[16,96,128]{2,1,0:T(8,128)(2,1)S(1)}, bf16[2,1536,128]{2,1,0:T(8,128)(2,1)S(1)}, bf16[2048,1536]{1,0:T(8,128)(2,1)S(1)}) custom-call(s32[1]{0:T(128)S(6)} %copy.14.base_ref, s32[16]{0:T(128)} %live_ref.1, bf16[96,4096]{1,0:T(8,128)(2,1)} %new_ref.1, bf16[2,96,4096]{2,1,0:T(8,128)(2,1)} %prev_ref.1, ...), custom_call_target="tpu_custom_call" | custom-call | tf_op jit(solution)/shard_map/compress/pallas_call | solution.py:292
  7.0 20.9 %all_to_all.10.got_ref = bf16[16,120,128]{2,1,0:T(8,128)(2,1)S(1)} all-to-all(bf16[16,120,128]{2,1,0:T(8,128)(2,1)S(1)} %get-tuple-element.10), channel_id=1, replica_groups=mesh['groups'=2,'tok'=16] {'tok'}, dimensions={0} | all-to-all | bytes 983040 | tf_op jit(solution)/shard_map/all_to_all | solution.py:318
  28.0 3.1 %attend.1 = bf16[512,128]{1,0:T(8,128)(2,1)S(1)} custom-call(bf16[16,96,128]{2,1,0:T(8,128)(2,1)S(1)} %get-tuple-element.9.dead_ref, bf16[16,120,128]{2,1,0:T(8,128)(2,1)S(1)} %all_to_all.10.got_ref, bf16[2,1536,128]{2,1,0:T(8,128)(2,1)S(1)} %get-tuple-element.11.cache_ref), custom_call_target="tpu_custom_call" | custom-call | tf_op jit(solution)/shard_map/attend/pallas_call | solution.py:323
  31.1 11.7 %all_to_all.11 = bf16[16,32,128]{2,1,0:T(8,128)(2,1)S(1)} all-to-all(bf16[16,32,128]{2,1,0:T(8,128)(2,1)S(1)} %bitcast.10), channel_id=1, replica_groups=mesh['groups'=2,'tok'=16] {'tok'}, dimensions={0} | all-to-all | bytes 262144 | tf_op jit(solution)/shard_map/all_to_all | solution.py:338
  42.8 0.1 copy.10
  42.9 1.8 %project.1 = bf16[32,1536]{1,0:T(8,128)(2,1)} custom-call(bf16[32,2048]{1,0:T(8,128)(2,1)S(1)} %bitcast.11, bf16[2048,1536]{1,0:T(8,128)(2,1)S(1)} %get-tuple-element.12.w_ref), custom_call_target="tpu_custom_call" | custom-call | tf_op jit(solution)/shard_map/project/pallas_call | solution.py:342
  (1 shorter events, 0.0 us)

commit v3 on v2

--- a/solution.py
+++ b/solution.py
@@ -135,23 +135,17 @@
                 block = q_buf[g * parts + j]
             out_ref[g * parts + j, q_at : q_at + block.shape[0], :] = block * bf16(HD**-0.5)
 
-    both_sums = [jnp.zeros((tokens + 2 * rank, 2 * tokens), f32)] * 2
+    total = jnp.zeros((tokens + 2 * rank, tokens), f32)
     for c in range(chunks):
         at = slice(c * step, (c + 1) * step)
         for copy in copies[c]:
             copy.wait()
-        delta = new_buf[c].astype(f32) - prev_buf[c].astype(f32)
-        high, low = split(delta)
+        high = (new_buf[c].astype(f32) - prev_buf[c].astype(f32)).astype(bf16)
         terms[:, at] = high
         s_high, s_low = split(sketch_buf[c])
-        lhs = jnp.concatenate([high, s_high, s_low], axis=0)
-        rhs = jnp.concatenate([high, low], axis=0)
-        for k in range(0, step, 256):
-            both_sums[(k // 256) % 2] = both_sums[(k // 256) % 2] + matmul(lhs[:, k : k + 256], rhs[:, k : k + 256], NT)
-    sums = both_sums[0] + both_sums[1]
-    total, cross = sums[:, :tokens], sums[:, tokens:]
-    gram = total[:tokens] + cross[:tokens] + cross[:tokens].T
-    y = total[tokens : tokens + rank] + total[tokens + rank :] + cross[tokens : tokens + rank]
+        total = total + matmul(jnp.concatenate([high, s_high, s_low], axis=0), high, NT)
+    gram = total[:tokens]
+    y = total[tokens : tokens + rank] + total[tokens + rank :]
 
     eye = jnp.where(
         lax.broadcasted_iota(jnp.int32, (tokens, tokens), 0) == lax.broadcasted_iota(jnp.int32, (tokens, tokens), 1),
@@ -222,21 +216,25 @@
         moved = q_rows if d == 0 else pltpu.roll(q_rows, LANES - d * HD, 1)
         q_all[d] = jnp.where(lane_q < HD, moved, jnp.where(lane_q == HD, 1.0, 0.0)).astype(bf16)
 
-    lane_o = lax.broadcasted_iota(jnp.int32, (block_rows, LANES), 1)
+    part = block_rows // 2
+    lane_o = lax.broadcasted_iota(jnp.int32, (part, LANES), 1)
 
     def one_block(b, carry):
-        at = pl.ds(pl.multiple_of(b * block_rows, block_rows), block_rows)
-        out = jnp.zeros((block_rows, LANES), f32)
+        start = b * block_rows
+        at = [pl.ds(start + i * part, part) for i in range(2)]
+        out = [None] * 2
         for d in range(per_dev):
-            scores = matmul(q_all[d, at, :], keys[d], NT)
-            exponent = jnp.exp(scores - jnp.max(scores, axis=1, keepdims=True)).astype(bf16)
-            sums = matmul(exponent, values[d], NN)
-            flipped = pltpu.roll(sums, HD, 1)
-            if d == 0:
-                out = flipped / sums
-            else:
-                out = jnp.where(lane_o < HD, out, sums / flipped)
-        out_ref[at, :] = out.astype(bf16)
+            scores = [matmul(q_all[d, at[i], :], keys[d], NT) for i in range(2)]
+            exponent = [jnp.exp(x - jnp.max(x, axis=1, keepdims=True)).astype(bf16) for x in scores]
+            for i in range(2):
+                sums = matmul(exponent[i], values[d], NN)
+                flipped = pltpu.roll(sums, HD, 1)
+                if d == 0:
+                    out[i] = flipped / sums
+                else:
+                    out[i] = jnp.where(lane_o < HD, out[i], sums / flipped)
+        for i in range(2):
+            out_ref[at[i], :] = out[i].astype(bf16)
         return carry
 
     count = shards * part_rows // block_rows

time: 44.9 us -> 43.6 us (0.971)
  Pallas kernels: 11.3 us -> 10 us
    pallas_call x1, Pallas kernels: 3.12 us -> 2.39 us  [per_device(): pl.pallas_call(functools.partial(attend_kernel, (per_dev, part_rows, rank...]
    pallas_call x1, Pallas kernels: 6.38 us -> 5.82 us  [per_device(): pl.pallas_call(functools.partial(compress_kernel, (per_dev, parts, part_r...]
where the time goes in v3:
time: 43.6 us; the launch traced here: 43.4 us
  blocking collectives  32.6 us (75%)
  Pallas kernels  10 us (23%)
  between operations  0.68 us (2%)
    all_to_all x1, blocking collectives, per_device(): got = lax.all_to_all(send, 'tok', split_axis=0, concat_axis=0, tiled=True)  20.9 us
    all_to_all x1, blocking collectives, per_device(): lax.all_to_all(attended, 'tok', split_axis=0, concat_axis=0, tiled=True)  11.7 us
    pallas_call x1, Pallas kernels, per_device(): pl.pallas_call(functools.partial(compress_kernel, (per_dev, parts, part_r...  5.82 us
    pallas_call x1, Pallas kernels, per_device(): pl.pallas_call(functools.partial(attend_kernel, (per_dev, part_rows, rank...  2.39 us
    pallas_call x1, Pallas kernels, per_device(): pl.pallas_call(project_kernel, out_shape=jax.ShapeDtypeStruct((query_rows...  1.82 us

profile of v3, /device:TPU:0, one launch (start us, length us, event | category | flops | bytes accessed | tf_op | source)
XLA Modules:
  0.0 43.4 jit_solution(13053103756964818013)
XLA Ops:
  0.7 5.8 %compress.1 = (bf16[16,120,128]{2,1,0:T(8,128)(2,1)S(1)}, bf16[16,96,128]{2,1,0:T(8,128)(2,1)S(1)}, bf16[2,1536,128]{2,1,0:T(8,128)(2,1)S(1)}, bf16[2048,1536]{1,0:T(8,128)(2,1)S(1)}) custom-call(s32[1]{0:T(128)S(6)} %copy.14.base_ref, s32[16]{0:T(128)} %live_ref.1, bf16[96,4096]{1,0:T(8,128)(2,1)} %new_ref.1, bf16[2,96,4096]{2,1,0:T(8,128)(2,1)} %prev_ref.1, ...), custom_call_target="tpu_custom_call" | custom-call | tf_op jit(solution)/shard_map/compress/pallas_call | solution.py:290
  6.5 20.9 %all_to_all.10.got_ref = bf16[16,120,128]{2,1,0:T(8,128)(2,1)S(1)} all-to-all(bf16[16,120,128]{2,1,0:T(8,128)(2,1)S(1)} %get-tuple-element.10), channel_id=1, replica_groups=mesh['groups'=2,'tok'=16] {'tok'}, dimensions={0} | all-to-all | bytes 983040 | tf_op jit(solution)/shard_map/all_to_all | solution.py:316
  27.4 2.4 %attend.1 = bf16[512,128]{1,0:T(8,128)(2,1)S(1)} custom-call(bf16[16,96,128]{2,1,0:T(8,128)(2,1)S(1)} %get-tuple-element.9.dead_ref, bf16[16,120,128]{2,1,0:T(8,128)(2,1)S(1)} %all_to_all.10.got_ref, bf16[2,1536,128]{2,1,0:T(8,128)(2,1)S(1)} %get-tuple-element.11.cache_ref), custom_call_target="tpu_custom_call" | custom-call | tf_op jit(solution)/shard_map/attend/pallas_call | solution.py:321
  29.8 11.7 %all_to_all.11 = bf16[16,32,128]{2,1,0:T(8,128)(2,1)S(1)} all-to-all(bf16[16,32,128]{2,1,0:T(8,128)(2,1)S(1)} %bitcast.10), channel_id=1, replica_groups=mesh['groups'=2,'tok'=16] {'tok'}, dimensions={0} | all-to-all | bytes 262144 | tf_op jit(solution)/shard_map/all_to_all | solution.py:336
  41.5 0.1 copy.10
  41.6 1.8 %project.1 = bf16[32,1536]{1,0:T(8,128)(2,1)} custom-call(bf16[32,2048]{1,0:T(8,128)(2,1)S(1)} %bitcast.11, bf16[2048,1536]{1,0:T(8,128)(2,1)S(1)} %get-tuple-element.12.w_ref), custom_call_target="tpu_custom_call" | custom-call | tf_op jit(solution)/shard_map/project/pallas_call | solution.py:340
  (1 shorter events, 0.0 us)

commit v4 on v3

--- a/solution.py
+++ b/solution.py
@@ -246,10 +246,14 @@
 
 def project_kernel(x_ref, w_ref, out_ref, buf, sems):
     chunks, rows, step = buf.shape
+    if x_ref.ndim == 3:
+        x = jnp.concatenate([x_ref[i] for i in range(x_ref.shape[0])], axis=1)
+    else:
+        x = x_ref[...]
     copies = []
     for c in range(chunks):
         at = slice(c * step, (c + 1) * step)
-        buf[c] = matmul(x_ref[...], w_ref[:, at], NN).astype(bf16)
+        buf[c] = matmul(x, w_ref[:, at], NN).astype(bf16)
         copies.append(pltpu.make_async_copy(buf.at[c], out_ref.at[:, pl.ds(c * step, step)], sems.at[c]))
         copies[c].start()
     for copy in copies:
@@ -334,8 +338,11 @@
     attended = attended.reshape(shards, part_rows, LANES)[:, :, :q_width]
 
     returned = lax.all_to_all(attended, "tok", split_axis=0, concat_axis=0, tiled=True)
-    returned = returned.reshape(groups, parts, part_rows, q_width)
-    row_block = returned.transpose(1, 2, 0, 3).reshape(query_rows, head_count * HD)
+    if parts == 1 and q_width == LANES:
+        row_block = returned
+    else:
+        returned = returned.reshape(groups, parts, part_rows, q_width)
+        row_block = returned.transpose(1, 2, 0, 3).reshape(query_rows, head_count * HD)
     chunks = 2
     return pl.pallas_call(
         project_kernel,

time: 43.6 us -> 43.5 us (level)
  no operation moved by 1% of the time
where the time goes in v4:
time: 43.5 us; the launch traced here: 43.3 us
  blocking collectives  32.6 us (75%)
  Pallas kernels  10 us (23%)
  between operations  0.67 us (2%)
    all_to_all x1, blocking collectives, per_device(): got = lax.all_to_all(send, 'tok', split_axis=0, concat_axis=0, tiled=True)  20.9 us
    all_to_all x1, blocking collectives, per_device(): lax.all_to_all(attended, 'tok', split_axis=0, concat_axis=0, tiled=True)  11.7 us
    pallas_call x1, Pallas kernels, per_device(): pl.pallas_call(functools.partial(compress_kernel, (per_dev, parts, part_r...  5.82 us
    pallas_call x1, Pallas kernels, per_device(): pl.pallas_call(functools.partial(attend_kernel, (per_dev, part_rows, rank...  2.39 us
    pallas_call x1, Pallas kernels, per_device(): pl.pallas_call(project_kernel, out_shape=jax.ShapeDtypeStruct((query_rows...  1.82 us

profile of v4, /device:TPU:0, one launch (start us, length us, event | category | flops | bytes accessed | tf_op | source)
XLA Modules:
  0.0 43.3 jit_solution(3091133191360972743)
XLA Ops:
  0.7 5.8 %compress.1 = (bf16[16,120,128]{2,1,0:T(8,128)(2,1)S(1)}, bf16[16,96,128]{2,1,0:T(8,128)(2,1)S(1)}, bf16[2,1536,128]{2,1,0:T(8,128)(2,1)S(1)}, bf16[2048,1536]{1,0:T(8,128)(2,1)S(1)}) custom-call(s32[1]{0:T(128)S(6)} %copy.9.base_ref, s32[16]{0:T(128)} %live_ref.1, bf16[96,4096]{1,0:T(8,128)(2,1)} %new_ref.1, bf16[2,96,4096]{2,1,0:T(8,128)(2,1)} %prev_ref.1, ...), custom_call_target="tpu_custom_call" | custom-call | tf_op jit(solution)/shard_map/compress/pallas_call | solution.py:294
  6.5 20.9 %all_to_all.10.got_ref = bf16[16,120,128]{2,1,0:T(8,128)(2,1)S(1)} all-to-all(bf16[16,120,128]{2,1,0:T(8,128)(2,1)S(1)} %get-tuple-element.10), channel_id=1, replica_groups=mesh['groups'=2,'tok'=16] {'tok'}, dimensions={0} | all-to-all | bytes 983040 | tf_op jit(solution)/shard_map/all_to_all | solution.py:320
  27.4 2.4 %attend.1 = bf16[512,128]{1,0:T(8,128)(2,1)S(1)} custom-call(bf16[16,96,128]{2,1,0:T(8,128)(2,1)S(1)} %get-tuple-element.9.dead_ref, bf16[16,120,128]{2,1,0:T(8,128)(2,1)S(1)} %all_to_all.10.got_ref, bf16[2,1536,128]{2,1,0:T(8,128)(2,1)S(1)} %get-tuple-element.11.cache_ref), custom_call_target="tpu_custom_call" | custom-call | tf_op jit(solution)/shard_map/attend/pallas_call | solution.py:325
  29.8 11.7 %all_to_all.11.x_ref = bf16[16,32,128]{2,1,0:T(8,128)(2,1)S(1)} all-to-all(bf16[16,32,128]{2,1,0:T(8,128)(2,1)S(1)} %bitcast.2), channel_id=1, replica_groups=mesh['groups'=2,'tok'=16] {'tok'}, dimensions={0} | all-to-all | bytes 262144 | tf_op jit(solution)/shard_map/all_to_all | solution.py:340
  41.5 1.8 %project.1 = bf16[32,1536]{1,0:T(8,128)(2,1)} custom-call(bf16[16,32,128]{2,1,0:T(8,128)(2,1)S(1)} %all_to_all.11.x_ref, bf16[2048,1536]{1,0:T(8,128)(2,1)S(1)} %get-tuple-element.12.w_ref), custom_call_target="tpu_custom_call" | custom-call | tf_op jit(solution)/shard_map/project/pallas_call | solution.py:347

commit v5 on v4

--- a/solution.py
+++ b/solution.py
@@ -223,8 +223,9 @@
         start = b * block_rows
         at = [pl.ds(start + i * part, part) for i in range(2)]
         out = [None] * 2
+        all_scores = [[matmul(q_all[d, at[i], :], keys[d], NT) for i in range(2)] for d in range(per_dev)]
         for d in range(per_dev):
-            scores = [matmul(q_all[d, at[i], :], keys[d], NT) for i in range(2)]
+            scores = all_scores[d]
             exponent = [jnp.exp(x - jnp.max(x, axis=1, keepdims=True)).astype(bf16) for x in scores]
             for i in range(2):
                 sums = matmul(exponent[i], values[d], NN)

time: 43.5 us -> 43.5 us (level)
  no operation moved by 1% of the time
where the time goes in v5:
time: 43.5 us; the launch traced here: 43.3 us
  blocking collectives  32.6 us (75%)
  Pallas kernels  10 us (23%)
  between operations  0.67 us (2%)
    all_to_all x1, blocking collectives, per_device(): got = lax.all_to_all(send, 'tok', split_axis=0, concat_axis=0, tiled=True)  20.9 us
    all_to_all x1, blocking collectives, per_device(): lax.all_to_all(attended, 'tok', split_axis=0, concat_axis=0, tiled=True)  11.7 us
    pallas_call x1, Pallas kernels, per_device(): pl.pallas_call(functools.partial(compress_kernel, (per_dev, parts, part_r...  5.82 us
    pallas_call x1, Pallas kernels, per_device(): pl.pallas_call(functools.partial(attend_kernel, (per_dev, part_rows, rank...  2.37 us
    pallas_call x1, Pallas kernels, per_device(): pl.pallas_call(project_kernel, out_shape=jax.ShapeDtypeStruct((query_rows...  1.82 us

profile of v5, /device:TPU:0, one launch (start us, length us, event | category | flops | bytes accessed | tf_op | source)
XLA Modules:
  0.0 43.3 jit_solution(17345954237173948423)
XLA Ops:
  0.7 5.8 %compress.1 = (bf16[16,120,128]{2,1,0:T(8,128)(2,1)S(1)}, bf16[16,96,128]{2,1,0:T(8,128)(2,1)S(1)}, bf16[2,1536,128]{2,1,0:T(8,128)(2,1)S(1)}, bf16[2048,1536]{1,0:T(8,128)(2,1)S(1)}) custom-call(s32[1]{0:T(128)S(6)} %copy.9.base_ref, s32[16]{0:T(128)} %live_ref.1, bf16[96,4096]{1,0:T(8,128)(2,1)} %new_ref.1, bf16[2,96,4096]{2,1,0:T(8,128)(2,1)} %prev_ref.1, ...), custom_call_target="tpu_custom_call" | custom-call | tf_op jit(solution)/shard_map/compress/pallas_call | solution.py:295
  6.5 20.9 %all_to_all.10.got_ref = bf16[16,120,128]{2,1,0:T(8,128)(2,1)S(1)} all-to-all(bf16[16,120,128]{2,1,0:T(8,128)(2,1)S(1)} %get-tuple-element.10), channel_id=1, replica_groups=mesh['groups'=2,'tok'=16] {'tok'}, dimensions={0} | all-to-all | bytes 983040 | tf_op jit(solution)/shard_map/all_to_all | solution.py:321
  27.4 2.4 %attend.1 = bf16[512,128]{1,0:T(8,128)(2,1)S(1)} custom-call(bf16[16,96,128]{2,1,0:T(8,128)(2,1)S(1)} %get-tuple-element.9.dead_ref, bf16[16,120,128]{2,1,0:T(8,128)(2,1)S(1)} %all_to_all.10.got_ref, bf16[2,1536,128]{2,1,0:T(8,128)(2,1)S(1)} %get-tuple-element.11.cache_ref), custom_call_target="tpu_custom_call" | custom-call | tf_op jit(solution)/shard_map/attend/pallas_call | solution.py:326
  29.8 11.7 %all_to_all.11.x_ref = bf16[16,32,128]{2,1,0:T(8,128)(2,1)S(1)} all-to-all(bf16[16,32,128]{2,1,0:T(8,128)(2,1)S(1)} %bitcast.2), channel_id=1, replica_groups=mesh['groups'=2,'tok'=16] {'tok'}, dimensions={0} | all-to-all | bytes 262144 | tf_op jit(solution)/shard_map/all_to_all | solution.py:341
  41.5 1.8 %project.1 = bf16[32,1536]{1,0:T(8,128)(2,1)} custom-call(bf16[16,32,128]{2,1,0:T(8,128)(2,1)S(1)} %all_to_all.11.x_ref, bf16[2048,1536]{1,0:T(8,128)(2,1)S(1)} %get-tuple-element.12.w_ref), custom_call_target="tpu_custom_call" | custom-call | tf_op jit(solution)/shard_map/project/pallas_call | solution.py:348
